TPU v7x, 256 devices: a whole 4x4x8 slice. The times are simulated.
256 devices in a mesh: row: 16 (over y, x), col: 2 (over core), ctx: 8 (over z).
Axes of the slice: x: 4, y: 4, z: 8, core: 2. Of those that a mesh axis runs over, the one named last changes fastest.
Arguments:
- queries: bfloat16 [8192, 6144], P(('col', 'ctx'), 'row'), may hold values from -16 to 16
- keys: bfloat16 [8192, 6144], P(('col', 'ctx'), 'row'), may hold values from -16 to 16
- values: bfloat16 [8192, 6144], P(('col', 'ctx'), 'row'), may hold values from -6 to 6
- out_weight: bfloat16 [6144, 6144], P('col', 'row'), may hold values from -0.078125 to 0.078125
- cotangent: bfloat16 [8192, 6144], P(('col', 'ctx'), 'row'), may hold values from -0.125 to 0.125
- block_mask: int32 [16, 16], replicated, may hold values from 0 to 1, as said below
Outputs:
- mixed_out: bfloat16 [8192, 6144], P(('col', 'ctx'), 'row')
- grad_weight: bfloat16 [6144, 6144], P(('col', 'ctx'), 'row')
Inputs may be any that keep to these rules, and one draw needn't show every extreme that they name: block_mask[i, i] is 1 for every block i, and block_mask[i, j] is 0 for j > i.
All inputs are finite; a program needn't handle non-finite values.
Results may differ from a plain program's by a relative error of at most 0.013.
Values may be sent and summed in bfloat16 or wider, within the bound.
A program may use at most 64 MiB of HBM per device.

v0:
```python
import math
import jax
import jax.numpy as jnp
from jax import lax
from jax.sharding import PartitionSpec as P

HD = 128
BLOCK = 512
NEGATIVE_FILL = -1e30


def attend_block(carried, query_heads, key_block, value_block, allowed, score_scale):
    run_max, run_sum, weighted = carried
    tok_rows, head_count, head_size = query_heads.shape
    key_heads = key_block.reshape(key_block.shape[0], head_count, head_size)
    value_heads = value_block.reshape(value_block.shape[0], head_count, head_size)
    scores = (
        jnp.einsum("thd,uhd->thu", query_heads, key_heads, preferred_element_type=jnp.float32)
        * score_scale
    )
    scores = jnp.where(allowed[:, None, None], scores, NEGATIVE_FILL)
    new_max = jnp.maximum(run_max, jnp.max(scores, axis=2))
    correction = jnp.exp(run_max - new_max)
    weights = jnp.where(allowed[:, None, None], jnp.exp(scores - new_max[:, :, None]), 0.0)
    new_sum = run_sum * correction + jnp.sum(weights, axis=2)
    product = jnp.einsum(
        "thu,uhd->thd",
        weights.astype(jnp.bfloat16),
        value_heads,
        preferred_element_type=jnp.float32,
    )
    new_weighted = weighted * correction[:, :, None] + product
    return (new_max, new_sum, new_weighted)


def body(queries, keys, values, out_weight, cotangent, block_mask):
    tok_rows, feature_width = queries.shape
    head_count = feature_width // HD
    query_heads = queries.reshape(tok_rows, head_count, HD)
    score_scale = 1.0 / math.sqrt(HD)
    local_blocks = tok_rows // BLOCK
    first_block = lax.axis_index(("col", "ctx")) * local_blocks
    local_mask = lax.dynamic_slice_in_dim(block_mask, first_block, local_blocks, 0)
    start_state = (
        jnp.full((tok_rows, head_count), NEGATIVE_FILL, jnp.float32),
        jnp.zeros((tok_rows, head_count), jnp.float32),
        jnp.zeros((tok_rows, head_count, HD), jnp.float32),
    )
    key_piece = lax.all_gather(keys, ("col", "ctx"), axis=0, tiled=True)
    value_piece = lax.all_gather(values, ("col", "ctx"), axis=0, tiled=True)
    block_count = key_piece.shape[0] // BLOCK
    key_stack = key_piece.reshape(block_count, BLOCK, feature_width)
    value_stack = value_piece.reshape(block_count, BLOCK, feature_width)
    block_columns = jnp.arange(block_count, dtype=jnp.int32)

    def one_block(state_in, entries):
        key_block, value_block, block_column = entries
        mask_column = lax.dynamic_index_in_dim(local_mask, block_column, 1, keepdims=False)
        allowed = jnp.repeat(mask_column, BLOCK, total_repeat_length=tok_rows) == 1
        updated = attend_block(state_in, query_heads, key_block, value_block, allowed, score_scale)
        return (updated, None)

    state_out, _ = lax.scan(one_block, start_state, (key_stack, value_stack, block_columns))
    run_max, run_sum, weighted = state_out
    attended = (
        (weighted / run_sum[:, :, None]).reshape(tok_rows, feature_width).astype(jnp.bfloat16)
    )
    all_heads = lax.all_gather(attended, "row", axis=1, tiled=True)
    head_columns = all_heads
    mixed_out = jnp.dot(
        head_columns,
        lax.all_gather(out_weight, "col", axis=0, tiled=True),
        preferred_element_type=jnp.float32,
    )
    head_columns = all_heads
    grad_weight = lax.psum_scatter(
        lax.dot_general(
            head_columns, cotangent, (((0,), (0,)), ((), ())), preferred_element_type=jnp.float32
        ),
        ("col", "ctx"),
        scatter_dimension=0,
        tiled=True,
    )
    return (mixed_out.astype(jnp.bfloat16), grad_weight.astype(jnp.bfloat16))


def solution(mesh):
    in_specs = (
        P(("col", "ctx"), "row"),
        P(("col", "ctx"), "row"),
        P(("col", "ctx"), "row"),
        P("col", "row"),
        P(("col", "ctx"), "row"),
        P(),
    )
    out_specs = (P(("col", "ctx"), "row"), P(("col", "ctx"), "row"))
    return jax.shard_map(body, mesh=mesh, in_specs=in_specs, out_specs=out_specs, check_vma=False)
```

profile of v0, /device:TPU:1, one launch (start us, length us, event | category | flops | bytes accessed | tf_op | source)
XLA Modules:
  0.0 622.6 jit_solution(9049366893125646251)
XLA Ops:
  12.0 48.1 %all-gather.5.cloned.1.call-done = bf16[8192,384]{1,0:T(8,128)(2,1)} async-done(((bf16[512,384]{1,0:T(8,128)(2,1)}), bf16[8192,384]{1,0:T(8,128)(2,1)}) %all-gather.5.cloned.1.call-update) | async-done | bytes 6291472 | tf_op jit(solution)/shard_map/all_gather | solution.py:49
  60.1 46.5 %all-gather.7.cloned.1.call-done = bf16[8192,384]{1,0:T(8,128)(2,1)} async-done(((bf16[512,384]{1,0:T(8,128)(2,1)}), bf16[8192,384]{1,0:T(8,128)(2,1)}) %all-gather.7.cloned.1.call-update) | async-done | bytes 6291472 | tf_op jit(solution)/shard_map/all_gather | solution.py:50
  107.2 304.6 %while.22 = (s32[]{:T(128)}, f32[512,3]{0,1:T(4,128)}, f32[512,3]{0,1:T(4,128)}, f32[512,3,128]{0,2,1:T(8,128)}, s32[16]{0:T(128)}, /*index=5*/s32[1,16]{1,0:T(1...) while((s32[]{:T(128)}, f32[512,3]{0,1:T(4,128)}, ...), condition=%wide.region_3.4_spmd.clone, body=%wide.region_0.3_spmd.clone.sunk | while | flops 413474304 | bytes 15433919 | solution.py:63
  111.5 1.9 constant_dynamic-slice_fusion.5
  114.3 2.4 bitcast_reduce_fusion.2
  118.7 1.9 copy.27
  120.7 3.4 fusion.42
  128.9 1.9 constant_dynamic-slice_fusion.5
  131.8 2.4 bitcast_reduce_fusion.2
  137.6 1.9 copy.27
  139.5 3.7 fusion.42
  148.1 1.9 constant_dynamic-slice_fusion.5
  151.0 2.4 bitcast_reduce_fusion.2
  156.8 1.9 copy.27
  158.7 3.7 fusion.42
  167.2 1.9 constant_dynamic-slice_fusion.5
  170.1 2.4 bitcast_reduce_fusion.2
  177.8 3.7 fusion.42
  186.4 1.9 constant_dynamic-slice_fusion.5
  189.2 2.4 bitcast_reduce_fusion.2
  197.0 3.7 fusion.42
  205.5 1.9 constant_dynamic-slice_fusion.5
  208.4 2.4 bitcast_reduce_fusion.2
  214.2 1.9 copy.27
  216.1 3.7 fusion.42
  224.6 1.9 constant_dynamic-slice_fusion.5
  227.5 2.4 bitcast_reduce_fusion.2
  235.2 3.7 fusion.42
  243.8 1.9 constant_dynamic-slice_fusion.5
  246.7 2.4 bitcast_reduce_fusion.2
  254.4 3.7 fusion.42
  262.9 1.9 constant_dynamic-slice_fusion.5
  265.8 2.4 bitcast_reduce_fusion.2
  273.5 3.7 fusion.42
  282.0 1.9 constant_dynamic-slice_fusion.5
  284.9 2.4 bitcast_reduce_fusion.2
  292.7 3.7 fusion.42
  301.2 1.9 constant_dynamic-slice_fusion.5
  304.1 2.4 bitcast_reduce_fusion.2
  311.8 3.7 fusion.42
  320.3 1.9 constant_dynamic-slice_fusion.5
  323.2 2.4 bitcast_reduce_fusion.2
  330.9 3.7 fusion.42
  339.5 1.9 constant_dynamic-slice_fusion.5
  342.4 2.4 bitcast_reduce_fusion.2
  348.1 1.9 copy.27
  350.1 3.7 fusion.42
  358.6 1.9 constant_dynamic-slice_fusion.5
  361.5 2.4 bitcast_reduce_fusion.2
  367.3 1.9 copy.27
  369.2 3.7 fusion.42
  377.7 1.9 constant_dynamic-slice_fusion.5
  380.6 2.4 bitcast_reduce_fusion.2
  388.3 3.7 fusion.42
  396.9 1.9 constant_dynamic-slice_fusion.5
  399.8 2.4 bitcast_reduce_fusion.2
  405.6 1.9 copy.27
  407.5 3.7 fusion.42
  411.7 2.0 divide_convert_fusion
  414.4 64.1 %all-gather.9.cloned.1.call-done = bf16[512,6144]{0,1:T(8,128)(2,1)} async-done(((bf16[512,384]{0,1:T(8,128)(2,1)}), bf16[512,6144]{0,1:T(8,128)(2,1)}) %all-gather.9.cloned.1.call-update) | async-done | bytes 6291472 | tf_op jit(solution)/shard_map/all_gather | solution.py:68
  478.5 9.9 %fusion.19 = f32[6144,384]{1,0:T(8,128)} fusion(bf16[512,6144]{0,1:T(8,128)(2,1)} %all-gather.9.cloned.1.call-done, bf16[512,384]{1,0:T(8,128)(2,1)S(1)} %copy-done), kind=kOutput, calls=%fused_computation.27 | convolution fusion | flops 2415919104 | bytes 16121856 | tf_op jit(solution)/shard_map/dot_general | solution.py:77
  488.4 12.0 %all-gather.11.cloned.1.call-done = bf16[6144,384]{1,0:T(8,128)(2,1)} async-done(((bf16[3072,384]{1,0:T(8,128)(2,1)}), bf16[6144,384]{1,0:T(8,128)(2,1)}) %all-gather.11.cloned.1.call-update) | async-done | bytes 4718608 | tf_op jit(solution)/shard_map/all_gather | solution.py:72
  500.4 8.3 %convolution_convert_fusion = bf16[512,384]{1,0:T(8,128)(2,1)} fusion(bf16[512,6144]{0,1:T(8,128)(2,1)} %all-gather.9.cloned.1.call-done, bf16[6144,384]{1,0:T(8,128)(2,1)} %all-gather.11.cloned.1.call-done), kind=kOutput, calls=%fused_computation.23 | convolution fusion | flops 2416115712 | bytes 11403264 | tf_op jit(solution)/shard_map/dot_general | solution.py:70
  508.7 105.5 %reduce-scatter.2.cloned.1.call-done = f32[384,384]{1,0:T(8,128)} async-done(((f32[6144,384]{1,0:T(8,128)}), f32[384,384]{1,0:T(8,128)}) %reduce-scatter.2.cloned.1.call-update) | async-done | bytes 589840 | tf_op jit(solution)/shard_map/reduce_scatter | solution.py:76
  (141 shorter events, 141.3 us)
Async XLA Ops:
  7.2 471.3 %copy-start = (bf16[512,384]{1,0:T(8,128)(2,1)S(1)}, bf16[512,384]{1,0:T(8,128)(2,1)}, u32[]{:S(2)}) copy-start(bf16[512,384]{1,0:T(8,128)(2,1)} %param.16) | copy-start | bytes 1179652
  7.2 53.0 %all-gather.5.cloned.1.call-start = ((), (), s32[]{:S(2)}) async-start(), calls=%async_computation.1 | async-start | bytes 6684672 | tf_op jit(solution)/shard_map/all_gather | solution.py:49
  7.9 98.7 %all-gather.7.cloned.1.call-start = ((), (), s32[]{:S(2)}) async-start(), calls=%async_computation.2 | async-start | bytes 6684672 | tf_op jit(solution)/shard_map/all_gather | solution.py:50
  8.7 469.8 %all-gather.9.cloned.1.call-start = ((), (), s32[]{:S(2)}) async-start(), calls=%async_computation.3 | async-start | bytes 6684672 | tf_op jit(solution)/shard_map/all_gather | solution.py:68
  413.7 86.7 %all-gather.11.cloned.1.call-start = ((), (), s32[]{:S(2)}) async-start(), calls=%async_computation.4 | async-start | bytes 7077888 | tf_op jit(solution)/shard_map/all_gather | solution.py:72
  414.3 200.0 %reduce-scatter.2.cloned.1.call-start = ((), (), s32[]{:S(2)}) async-start(), calls=%async_computation.5 | async-start | bytes 10027008 | tf_op jit(solution)/shard_map/reduce_scatter | solution.py:76
Sparse Core Ops, SparseCore 0:
  9.8 50.2 all-gather.4
  62.0 44.6 all-gather.6
  413.9 64.5 all-gather.8
  480.1 20.2 all-gather.10
  502.8 111.4 reduce-scatter.1
where the time goes:
time: 627 us; the launch traced here: 623 us
  waiting for transfers between devices  278 us (44%)
  matrix products  115 us (18%)
  local copies, waits for them, and re-layouts  110 us (18%)
  other arithmetic  75.8 us (12%)
  loops' own time  29.9 us (5%)
  between operations  13.8 us (2%)
    reduce_scatter x1, waiting for transfers between devices, body(): lax.psum_scatter(lax.dot_general(head_columns, cotangent, (((0,), (0,)),...  106 us
    dynamic_slice x64, local copies, waits for them, and re-layouts, body(): lax.scan(one_block, start_state, (key_stack, value_stack, block_columns))  96.5 us
    all_gather x1, waiting for transfers between devices, body(): all_heads = lax.all_gather(attended, 'row', axis=1, tiled=True)  64.1 us
    dot_general x16, matrix products, attend_block(): jnp.einsum('thu,uhd->thd', weights.astype(jnp.bfloat16), value_heads, pre...  58.4 us
    all_gather x1, waiting for transfers between devices, body(): key_piece = lax.all_gather(keys, ('col', 'ctx'), axis=0, tiled=True)  48.1 us
    all_gather x1, waiting for transfers between devices, body(): value_piece = lax.all_gather(values, ('col', 'ctx'), axis=0, tiled=True)  46.5 us
    dot_general x16, matrix products, attend_block(): jnp.einsum('thd,uhd->thu', query_heads, key_heads, preferred_element_type...  38.2 us
    another operation x1, loops' own time, body(): lax.scan(one_block, start_state, (key_stack, value_stack, block_columns))  29.9 us
  transfers between devices with their start and end apart: 5, of which 5 were waited for; matrix products, arithmetic and copies ran while one was open for 3% of the time, Pallas kernels for 0%

commit v1 on v0

--- a/solution.py
+++ b/solution.py
@@ -65,7 +65,12 @@
     attended = (
         (weighted / run_sum[:, :, None]).reshape(tok_rows, feature_width).astype(jnp.bfloat16)
     )
-    all_heads = lax.all_gather(attended, "row", axis=1, tiled=True)
+    ring = [attended]
+    for hop in range(15):
+        ring.append(lax.ppermute(ring[-1], "row", [(dev, (dev + 1) % 16) for dev in range(16)]))
+    all_heads = jnp.roll(
+        jnp.concatenate(ring[::-1], axis=1), (lax.axis_index("row") + 1) * ring[0].shape[1], axis=1
+    )
     head_columns = all_heads
     mixed_out = jnp.dot(
         head_columns,

time: 627 us -> 752 us (1.20)
  waiting for transfers between devices: 278 us -> 383 us
  local copies, waits for them, and re-layouts: 110 us -> 132 us
    ppermute x0 -> x15, waiting for transfers between devices: none -> 176 us  [body(): lax.ppermute(ring[-1], 'row', [(dev, (dev + 1) % 16) for dev in range(16)])]
    all_gather x1 -> x0, waiting for transfers between devices: 64.1 us -> none  [body(): all_heads = lax.all_gather(attended, 'row', axis=1, tiled=True)]
    unnamed x4 -> x61, local copies, waits for them, and re-layouts: 2.1 us -> 22.9 us
    all_gather x1, waiting for transfers between devices: 12 us -> 0.03 us  [body(): lax.all_gather(out_weight, 'col', axis=0, tiled=True)]
  transfers between devices with their start and end apart: 5 -> 19, of which waited for: 5 -> 18; matrix products, arithmetic and copies ran while one was open for 3% -> 4% of each run, Pallas kernels for 0% -> 0%
where the time goes in v1:
time: 752 us; the launch traced here: 747 us
  waiting for transfers between devices  383 us (51%)
  local copies, waits for them, and re-layouts  132 us (18%)
  matrix products  110 us (15%)
  other arithmetic  76 us (10%)
  loops' own time  29.4 us (4%)
  between operations  15.6 us (2%)
    ppermute x15, waiting for transfers between devices, body(): lax.ppermute(ring[-1], 'row', [(dev, (dev + 1) % 16) for dev in range(16)])  176 us
    reduce_scatter x1, waiting for transfers between devices, body(): lax.psum_scatter(lax.dot_general(head_columns, cotangent, (((0,), (0,)),...  110 us
    dynamic_slice x64, local copies, waits for them, and re-layouts, body(): lax.scan(one_block, start_state, (key_stack, value_stack, block_columns))  97.5 us
    dot_general x16, matrix products, attend_block(): jnp.einsum('thu,uhd->thd', weights.astype(jnp.bfloat16), value_heads, pre...  57.7 us
    all_gather x1, waiting for transfers between devices, body(): key_piece = lax.all_gather(keys, ('col', 'ctx'), axis=0, tiled=True)  48 us
    all_gather x1, waiting for transfers between devices, body(): value_piece = lax.all_gather(values, ('col', 'ctx'), axis=0, tiled=True)  46.5 us
    dot_general x16, matrix products, attend_block(): jnp.einsum('thd,uhd->thu', query_heads, key_heads, preferred_element_type...  38.1 us
    another operation x1, loops' own time, body(): lax.scan(one_block, start_state, (key_stack, value_stack, block_columns))  29.4 us
  transfers between devices with their start and end apart: 19, of which 18 were waited for; matrix products, arithmetic and copies ran while one was open for 4% of the time, Pallas kernels for 0%

profile of v1, /device:TPU:1, one launch (start us, length us, event | category | flops | bytes accessed | tf_op | source)
XLA Modules:
  0.0 747.0 jit_solution(2190986435963714831)
XLA Ops:
  12.9 48.0 %all-gather.4.cloned.1.call-done = bf16[8192,384]{1,0:T(8,128)(2,1)} async-done(((bf16[512,384]{1,0:T(8,128)(2,1)}), bf16[8192,384]{1,0:T(8,128)(2,1)}) %all-gather.4.cloned.1.call-update) | async-done | bytes 6291472 | tf_op jit(solution)/shard_map/all_gather | solution.py:49
  61.0 46.5 %all-gather.6.cloned.1.call-done = bf16[8192,384]{1,0:T(8,128)(2,1)} async-done(((bf16[512,384]{1,0:T(8,128)(2,1)}), bf16[8192,384]{1,0:T(8,128)(2,1)}) %all-gather.6.cloned.1.call-update) | async-done | bytes 6291472 | tf_op jit(solution)/shard_map/all_gather | solution.py:50
  108.1 305.2 %while.22 = (s32[]{:T(128)}, f32[512,3]{0,1:T(4,128)}, f32[512,3]{0,1:T(4,128)}, f32[512,3,128]{0,2,1:T(8,128)}, s32[16]{0:T(128)}, /*index=5*/s32[1,16]{1,0:T(1...) while((s32[]{:T(128)}, f32[512,3]{0,1:T(4,128)}, ...), condition=%wide.region_3.4_spmd.clone, body=%wide.region_0.3_spmd.clone.sunk | while | flops 413474304 | bytes 15433919 | solution.py:63
  112.4 1.9 constant_dynamic-slice_fusion.5
  115.3 2.4 bitcast_reduce_fusion.2
  121.6 3.4 fusion.48
  130.0 1.9 constant_dynamic-slice_fusion.5
  132.9 2.4 bitcast_reduce_fusion.2
  140.5 3.6 fusion.48
  149.1 1.9 constant_dynamic-slice_fusion.5
  152.0 2.4 bitcast_reduce_fusion.2
  159.7 3.6 fusion.48
  168.3 1.9 constant_dynamic-slice_fusion.5
  171.2 2.4 bitcast_reduce_fusion.2
  178.9 3.6 fusion.48
  187.5 1.9 constant_dynamic-slice_fusion.5
  190.4 2.4 bitcast_reduce_fusion.2
  198.1 3.6 fusion.48
  206.7 1.9 constant_dynamic-slice_fusion.5
  209.6 2.4 bitcast_reduce_fusion.2
  217.3 3.6 fusion.48
  225.9 1.9 constant_dynamic-slice_fusion.5
  228.8 2.4 bitcast_reduce_fusion.2
  236.4 3.6 fusion.48
  245.0 1.9 constant_dynamic-slice_fusion.5
  247.9 2.4 bitcast_reduce_fusion.2
  255.6 3.6 fusion.48
  264.2 1.9 constant_dynamic-slice_fusion.5
  267.1 2.4 bitcast_reduce_fusion.2
  274.8 3.6 fusion.48
  283.4 1.9 constant_dynamic-slice_fusion.5
  286.3 2.4 bitcast_reduce_fusion.2
  294.0 3.6 fusion.48
  305.5 2.4 bitcast_reduce_fusion.2
  313.2 3.6 fusion.48
  324.6 2.4 bitcast_reduce_fusion.2
  332.3 3.6 fusion.48
  343.8 2.4 bitcast_reduce_fusion.2
  351.5 3.6 fusion.48
  363.0 2.4 bitcast_reduce_fusion.2
  370.7 3.6 fusion.48
  382.2 2.4 bitcast_reduce_fusion.2
  389.9 3.6 fusion.48
  401.4 2.4 bitcast_reduce_fusion.2
  409.1 3.6 fusion.48
  415.8 12.6 %collective-permute-done = bf16[512,384]{0,1:T(8,128)(2,1)S(1)} collective-permute-done((bf16[512,384]{0,1:T(8,128)(2,1)S(1)}, bf16[512,384]{0,1:T(8,128)(2,1)S(1)}, u32[]{:S(2)}, u32[]{:S(2)}) %collective-permute-start) | collective-permute-done | bytes 393248 | tf_op jit(solution)/shard_map/ppermute | solution.py:70
  428.3 12.8 %collective-permute-done.1 = bf16[512,384]{0,1:T(8,128)(2,1)S(1)} collective-permute-done((bf16[512,384]{0,1:T(8,128)(2,1)S(1)}, bf16[512,384]{0,1:T(8,128)(2,1)S(1)}, u32[]{:S(2)}, u32[]{:S(2)}) %collective-permute-start.1) | collective-permute-done | bytes 393248 | tf_op jit(solution)/shard_map/ppermute | solution.py:70
  441.2 11.9 %collective-permute-done.2 = bf16[512,384]{0,1:T(8,128)(2,1)S(1)} collective-permute-done((bf16[512,384]{0,1:T(8,128)(2,1)S(1)}, bf16[512,384]{0,1:T(8,128)(2,1)S(1)}, u32[]{:S(2)}, u32[]{:S(2)}) %collective-permute-start.2) | collective-permute-done | bytes 393248 | tf_op jit(solution)/shard_map/ppermute | solution.py:70
  453.1 11.0 %collective-permute-done.3 = bf16[512,384]{0,1:T(8,128)(2,1)S(1)} collective-permute-done((bf16[512,384]{0,1:T(8,128)(2,1)S(1)}, bf16[512,384]{0,1:T(8,128)(2,1)S(1)}, u32[]{:S(2)}, u32[]{:S(2)}) %collective-permute-start.3) | collective-permute-done | bytes 393248 | tf_op jit(solution)/shard_map/ppermute | solution.py:70
  464.1 9.9 %collective-permute-done.4 = bf16[512,384]{0,1:T(8,128)(2,1)S(1)} collective-permute-done((bf16[512,384]{0,1:T(8,128)(2,1)S(1)}, bf16[512,384]{0,1:T(8,128)(2,1)S(1)}, u32[]{:S(2)}, u32[]{:S(2)}) %collective-permute-start.4) | collective-permute-done | bytes 393248 | tf_op jit(solution)/shard_map/ppermute | solution.py:70
  474.1 9.9 %collective-permute-done.5 = bf16[512,384]{0,1:T(8,128)(2,1)S(1)} collective-permute-done((bf16[512,384]{0,1:T(8,128)(2,1)S(1)}, bf16[512,384]{0,1:T(8,128)(2,1)S(1)}, u32[]{:S(2)}, u32[]{:S(2)}) %collective-permute-start.5) | collective-permute-done | bytes 393248 | tf_op jit(solution)/shard_map/ppermute | solution.py:70
  484.0 9.9 %collective-permute-done.6 = bf16[512,384]{0,1:T(8,128)(2,1)S(1)} collective-permute-done((bf16[512,384]{0,1:T(8,128)(2,1)S(1)}, bf16[512,384]{0,1:T(8,128)(2,1)S(1)}, u32[]{:S(2)}, u32[]{:S(2)}) %collective-permute-start.6) | collective-permute-done | bytes 393248 | tf_op jit(solution)/shard_map/ppermute | solution.py:70
  494.0 10.8 %collective-permute-done.7 = bf16[512,384]{0,1:T(8,128)(2,1)S(1)} collective-permute-done((bf16[512,384]{0,1:T(8,128)(2,1)S(1)}, bf16[512,384]{0,1:T(8,128)(2,1)S(1)}, u32[]{:S(2)}, u32[]{:S(2)}) %collective-permute-start.7) | collective-permute-done | bytes 393248 | tf_op jit(solution)/shard_map/ppermute | solution.py:70
  505.5 11.2 %collective-permute-done.8 = bf16[512,384]{0,1:T(8,128)(2,1)S(1)} collective-permute-done((bf16[512,384]{0,1:T(8,128)(2,1)S(1)}, bf16[512,384]{0,1:T(8,128)(2,1)S(1)}, u32[]{:S(2)}, u32[]{:S(2)}) %collective-permute-start.8) | collective-permute-done | bytes 393248 | tf_op jit(solution)/shard_map/ppermute | solution.py:70
  517.4 12.2 %collective-permute-done.9 = bf16[512,384]{0,1:T(8,128)(2,1)S(1)} collective-permute-done((bf16[512,384]{0,1:T(8,128)(2,1)S(1)}, bf16[512,384]{0,1:T(8,128)(2,1)S(1)}, u32[]{:S(2)}, u32[]{:S(2)}) %collective-permute-start.9) | collective-permute-done | bytes 393248 | tf_op jit(solution)/shard_map/ppermute | solution.py:70
  530.4 13.3 %collective-permute-done.10 = bf16[512,384]{0,1:T(8,128)(2,1)S(1)} collective-permute-done((bf16[512,384]{0,1:T(8,128)(2,1)S(1)}, bf16[512,384]{0,1:T(8,128)(2,1)S(1)}, u32[]{:S(2)}, u32[]{:S(2)}) %collective-permute-start.10) | collective-permute-done | bytes 393248 | tf_op jit(solution)/shard_map/ppermute | solution.py:70
  544.5 14.1 %collective-permute-done.11 = bf16[512,384]{0,1:T(8,128)(2,1)S(1)} collective-permute-done((bf16[512,384]{0,1:T(8,128)(2,1)S(1)}, bf16[512,384]{0,1:T(8,128)(2,1)S(1)}, u32[]{:S(2)}, u32[]{:S(2)}) %collective-permute-start.11) | collective-permute-done | bytes 393248 | tf_op jit(solution)/shard_map/ppermute | solution.py:70
  559.3 13.2 %collective-permute-done.12 = bf16[512,384]{0,1:T(8,128)(2,1)S(1)} collective-permute-done((bf16[512,384]{0,1:T(8,128)(2,1)S(1)}, bf16[512,384]{0,1:T(8,128)(2,1)S(1)}, u32[]{:S(2)}, u32[]{:S(2)}) %collective-permute-start.12) | collective-permute-done | bytes 393248 | tf_op jit(solution)/shard_map/ppermute | solution.py:70
  573.3 12.3 %collective-permute-done.13 = bf16[512,384]{0,1:T(8,128)(2,1)} collective-permute-done((bf16[512,384]{0,1:T(8,128)(2,1)S(1)}, bf16[512,384]{0,1:T(8,128)(2,1)}, u32[]{:S(2)}, u32[]{:S(2)}) %collective-permute-start.13) | collective-permute-done | bytes 393248 | tf_op jit(solution)/shard_map/ppermute | solution.py:70
  585.8 11.0 %collective-permute-done.14 = bf16[512,384]{0,1:T(8,128)(2,1)} collective-permute-done((bf16[512,384]{0,1:T(8,128)(2,1)}, bf16[512,384]{0,1:T(8,128)(2,1)}, u32[]{:S(2)}, u32[]{:S(2)}) %collective-permute-start.14) | collective-permute-done | bytes 393248 | tf_op jit(solution)/shard_map/ppermute | solution.py:70
  607.9 5.5 copy-done.1
  613.4 5.8 fusion.18
  619.3 8.4 %fusion.22 = bf16[512,384]{1,0:T(8,128)(2,1)} fusion(bf16[6144,384]{1,0:T(8,128)(2,1)} %all-gather.8.cloned.1.call-done, bf16[512,12288]{0,1:T(8,128)(2,1)} %copy-done.1, s32[]{:T(128)S(6)} %select_n.86), kind=kOutput, calls=%fused_computation.27 | convolution fusion | flops 2416115712 | bytes 11403268 | tf_op jit(solution)/shard_map/dot_general | solution.py:75
  627.7 110.4 %reduce-scatter.2.cloned.1.call-done = f32[384,384]{1,0:T(8,128)} async-done(((f32[6144,384]{1,0:T(8,128)}), f32[384,384]{1,0:T(8,128)}) %reduce-scatter.2.cloned.1.call-update) | async-done | bytes 589840 | tf_op jit(solution)/shard_map/reduce_scatter | solution.py:81
  (226 shorter events, 185.8 us)
Async XLA Ops:
  8.0 605.4 %copy-start = (bf16[512,384]{1,0:T(8,128)(2,1)S(1)}, bf16[512,384]{1,0:T(8,128)(2,1)}, u32[]{:S(2)}) copy-start(bf16[512,384]{1,0:T(8,128)(2,1)} %param.16) | copy-start | bytes 1179652
  8.0 53.0 %all-gather.4.cloned.1.call-start = ((), (), s32[]{:S(2)}) async-start(), calls=%async_computation.1 | async-start | bytes 6684672 | tf_op jit(solution)/shard_map/all_gather | solution.py:49
  8.7 98.7 %all-gather.6.cloned.1.call-start = ((), (), s32[]{:S(2)}) async-start(), calls=%async_computation.2 | async-start | bytes 6684672 | tf_op jit(solution)/shard_map/all_gather | solution.py:50
  9.5 609.8 %all-gather.8.cloned.1.call-start = ((), (), s32[]{:S(2)}) async-start(), calls=%async_computation.3 | async-start | bytes 7077888 | tf_op jit(solution)/shard_map/all_gather | solution.py:77
  414.5 13.8 %collective-permute-start = (bf16[512,384]{0,1:T(8,128)(2,1)S(1)}, bf16[512,384]{0,1:T(8,128)(2,1)S(1)}, u32[]{:S(2)}, u32[]{:S(2)}) collective-permute-start(bf16[512,384]{0,1:T(8,128)(2,1)S(1)} %bitcast.57), channel_id=1, source_target_pairs={{0,16},{16,32},{32,48},{48,64},{64,80},{80,96},{96,112},{112,128},... | collective-permute-start | bytes 1179656 | tf_op jit(solution)/shard_map/ppermute | solution.py:70
  428.3 12.8 %collective-permute-start.1 = (bf16[512,384]{0,1:T(8,128)(2,1)S(1)}, bf16[512,384]{0,1:T(8,128)(2,1)S(1)}, u32[]{:S(2)}, u32[]{:S(2)}) collective-permute-start(bf16[512,384]{0,1:T(8,128)(2,1)S(1)} %collective-permute-done), channel_id=1, source_target_pairs={{0,16},{16,32},{32,48},{48,64},{64,80},{80,96},{96,112},{112,128},... | collective-permute-start | bytes 1179656 | tf_op jit(solution)/shard_map/ppermute | solution.py:70
  441.2 11.9 %collective-permute-start.2 = (bf16[512,384]{0,1:T(8,128)(2,1)S(1)}, bf16[512,384]{0,1:T(8,128)(2,1)S(1)}, u32[]{:S(2)}, u32[]{:S(2)}) collective-permute-start(bf16[512,384]{0,1:T(8,128)(2,1)S(1)} %collective-permute-done.1), channel_id=1, source_target_pairs={{0,16},{16,32},{32,48},{48,64},{64,80},{80,96},{96,112},{112,128},... | collective-permute-start | bytes 1179656 | tf_op jit(solution)/shard_map/ppermute | solution.py:70
  453.1 11.0 %collective-permute-start.3 = (bf16[512,384]{0,1:T(8,128)(2,1)S(1)}, bf16[512,384]{0,1:T(8,128)(2,1)S(1)}, u32[]{:S(2)}, u32[]{:S(2)}) collective-permute-start(bf16[512,384]{0,1:T(8,128)(2,1)S(1)} %collective-permute-done.2), channel_id=1, source_target_pairs={{0,16},{16,32},{32,48},{48,64},{64,80},{80,96},{96,112},{112,128},... | collective-permute-start | bytes 1179656 | tf_op jit(solution)/shard_map/ppermute | solution.py:70
  464.1 9.9 %collective-permute-start.4 = (bf16[512,384]{0,1:T(8,128)(2,1)S(1)}, bf16[512,384]{0,1:T(8,128)(2,1)S(1)}, u32[]{:S(2)}, u32[]{:S(2)}) collective-permute-start(bf16[512,384]{0,1:T(8,128)(2,1)S(1)} %collective-permute-done.3), channel_id=1, source_target_pairs={{0,16},{16,32},{32,48},{48,64},{64,80},{80,96},{96,112},{112,128},... | collective-permute-start | bytes 1179656 | tf_op jit(solution)/shard_map/ppermute | solution.py:70
  474.1 9.9 %collective-permute-start.5 = (bf16[512,384]{0,1:T(8,128)(2,1)S(1)}, bf16[512,384]{0,1:T(8,128)(2,1)S(1)}, u32[]{:S(2)}, u32[]{:S(2)}) collective-permute-start(bf16[512,384]{0,1:T(8,128)(2,1)S(1)} %collective-permute-done.4), channel_id=1, source_target_pairs={{0,16},{16,32},{32,48},{48,64},{64,80},{80,96},{96,112},{112,128},... | collective-permute-start | bytes 1179656 | tf_op jit(solution)/shard_map/ppermute | solution.py:70
  484.0 9.9 %collective-permute-start.6 = (bf16[512,384]{0,1:T(8,128)(2,1)S(1)}, bf16[512,384]{0,1:T(8,128)(2,1)S(1)}, u32[]{:S(2)}, u32[]{:S(2)}) collective-permute-start(bf16[512,384]{0,1:T(8,128)(2,1)S(1)} %collective-permute-done.5), channel_id=1, source_target_pairs={{0,16},{16,32},{32,48},{48,64},{64,80},{80,96},{96,112},{112,128},... | collective-permute-start | bytes 1179656 | tf_op jit(solution)/shard_map/ppermute | solution.py:70
  494.0 10.8 %collective-permute-start.7 = (bf16[512,384]{0,1:T(8,128)(2,1)S(1)}, bf16[512,384]{0,1:T(8,128)(2,1)S(1)}, u32[]{:S(2)}, u32[]{:S(2)}) collective-permute-start(bf16[512,384]{0,1:T(8,128)(2,1)S(1)} %collective-permute-done.6), channel_id=1, source_target_pairs={{0,16},{16,32},{32,48},{48,64},{64,80},{80,96},{96,112},{112,128},... | collective-permute-start | bytes 1179656 | tf_op jit(solution)/shard_map/ppermute | solution.py:70
  504.8 0.7 copy-start.2
  505.5 11.2 %collective-permute-start.8 = (bf16[512,384]{0,1:T(8,128)(2,1)S(1)}, bf16[512,384]{0,1:T(8,128)(2,1)S(1)}, u32[]{:S(2)}, u32[]{:S(2)}) collective-permute-start(bf16[512,384]{0,1:T(8,128)(2,1)S(1)} %collective-permute-done.7), channel_id=1, source_target_pairs={{0,16},{16,32},{32,48},{48,64},{64,80},{80,96},{96,112},{112,128},... | collective-permute-start | bytes 1179656 | tf_op jit(solution)/shard_map/ppermute | solution.py:70
  516.7 0.8 copy-start.4
  517.4 12.2 %collective-permute-start.9 = (bf16[512,384]{0,1:T(8,128)(2,1)S(1)}, bf16[512,384]{0,1:T(8,128)(2,1)S(1)}, u32[]{:S(2)}, u32[]{:S(2)}) collective-permute-start(bf16[512,384]{0,1:T(8,128)(2,1)S(1)} %collective-permute-done.8), channel_id=1, source_target_pairs={{0,16},{16,32},{32,48},{48,64},{64,80},{80,96},{96,112},{112,128},... | collective-permute-start | bytes 1179656 | tf_op jit(solution)/shard_map/ppermute | solution.py:70
  529.7 0.8 copy-start.6
  530.4 13.3 %collective-permute-start.10 = (bf16[512,384]{0,1:T(8,128)(2,1)S(1)}, bf16[512,384]{0,1:T(8,128)(2,1)S(1)}, u32[]{:S(2)}, u32[]{:S(2)}) collective-permute-start(bf16[512,384]{0,1:T(8,128)(2,1)S(1)} %collective-permute-done.9), channel_id=1, source_target_pairs={{0,16},{16,32},{32,48},{48,64},{64,80},{80,96},{96,112},{112,128},... | collective-permute-start | bytes 1179656 | tf_op jit(solution)/shard_map/ppermute | solution.py:70
  543.7 0.7 copy-start.8
  544.5 14.1 %collective-permute-start.11 = (bf16[512,384]{0,1:T(8,128)(2,1)S(1)}, bf16[512,384]{0,1:T(8,128)(2,1)S(1)}, u32[]{:S(2)}, u32[]{:S(2)}) collective-permute-start(bf16[512,384]{0,1:T(8,128)(2,1)S(1)} %collective-permute-done.10), channel_id=1, source_target_pairs={{0,16},{16,32},{32,48},{48,64},{64,80},{80,96},{96,112},{112,128},... | collective-permute-start | bytes 1179656 | tf_op jit(solution)/shard_map/ppermute | solution.py:70
  558.6 0.7 copy-start.10
  559.3 13.2 %collective-permute-start.12 = (bf16[512,384]{0,1:T(8,128)(2,1)S(1)}, bf16[512,384]{0,1:T(8,128)(2,1)S(1)}, u32[]{:S(2)}, u32[]{:S(2)}) collective-permute-start(bf16[512,384]{0,1:T(8,128)(2,1)S(1)} %collective-permute-done.11), channel_id=1, source_target_pairs={{0,16},{16,32},{32,48},{48,64},{64,80},{80,96},{96,112},{112,128},... | collective-permute-start | bytes 1179656 | tf_op jit(solution)/shard_map/ppermute | solution.py:70
  572.6 0.7 copy-start.12
  573.3 12.3 %collective-permute-start.13 = (bf16[512,384]{0,1:T(8,128)(2,1)S(1)}, bf16[512,384]{0,1:T(8,128)(2,1)}, u32[]{:S(2)}, u32[]{:S(2)}) collective-permute-start(bf16[512,384]{0,1:T(8,128)(2,1)S(1)} %collective-permute-done.12), channel_id=1, source_target_pairs={{0,16},{16,32},{32,48},{48,64},{64,80},{80,96},{96,112},{112,128},... | collective-permute-start | bytes 1179656 | tf_op jit(solution)/shard_map/ppermute | solution.py:70
  585.6 11.2 %collective-permute-start.14 = (bf16[512,384]{0,1:T(8,128)(2,1)}, bf16[512,384]{0,1:T(8,128)(2,1)}, u32[]{:S(2)}, u32[]{:S(2)}) collective-permute-start(bf16[512,384]{0,1:T(8,128)(2,1)} %collective-permute-done.13), channel_id=1, source_target_pairs={{0,16},{16,32},{32,48},{48,64},{64,80},{80,96},{96,112},{112,128},... | collective-permute-start | bytes 1179656 | tf_op jit(solution)/shard_map/ppermute | solution.py:70
  585.7 152.4 %reduce-scatter.2.cloned.1.call-start = ((), (), s32[]{:S(2)}) async-start(), calls=%async_computation.4 | async-start | bytes 10027008 | tf_op jit(solution)/shard_map/reduce_scatter | solution.py:81
  585.7 21.6 %copy-start.13 = (bf16[512,384]{0,1:T(8,128)(2,1)S(1)}, bf16[512,384]{0,1:T(8,128)(2,1)}, u32[]{:S(2)}) copy-start(bf16[512,384]{0,1:T(8,128)(2,1)} %copy-done.12) | copy-start | bytes 1179652
  585.7 21.7 %copy-start.11 = (bf16[512,384]{0,1:T(8,128)(2,1)S(1)}, bf16[512,384]{0,1:T(8,128)(2,1)}, u32[]{:S(2)}) copy-start(bf16[512,384]{0,1:T(8,128)(2,1)} %copy-done.10) | copy-start | bytes 1179652
  585.8 21.7 %copy-start.9 = (bf16[512,384]{0,1:T(8,128)(2,1)S(1)}, bf16[512,384]{0,1:T(8,128)(2,1)}, u32[]{:S(2)}) copy-start(bf16[512,384]{0,1:T(8,128)(2,1)} %copy-done.8) | copy-start | bytes 1179652
  585.8 21.7 %copy-start.7 = (bf16[512,384]{0,1:T(8,128)(2,1)S(1)}, bf16[512,384]{0,1:T(8,128)(2,1)}, u32[]{:S(2)}) copy-start(bf16[512,384]{0,1:T(8,128)(2,1)} %copy-done.6) | copy-start | bytes 1179652
  585.8 21.8 %copy-start.5 = (bf16[512,384]{0,1:T(8,128)(2,1)S(1)}, bf16[512,384]{0,1:T(8,128)(2,1)}, u32[]{:S(2)}) copy-start(bf16[512,384]{0,1:T(8,128)(2,1)} %copy-done.4) | copy-start | bytes 1179652
  585.8 21.8 %copy-start.3 = (bf16[512,384]{0,1:T(8,128)(2,1)S(1)}, bf16[512,384]{0,1:T(8,128)(2,1)}, u32[]{:S(2)}) copy-start(bf16[512,384]{0,1:T(8,128)(2,1)} %copy-done.2) | copy-start | bytes 1179652
  607.9 5.5 copy-start.1
Sparse Core Ops, SparseCore 0:
  10.7 50.2 all-gather.3
  62.8 44.6 all-gather.5
  619.4 118.6 reduce-scatter.1
Sparse Core Ops, SparseCore 1:
  585.7 33.4 all-gather.7
